TPU v7x, 256 devices: a whole 4x4x8 slice. The times are simulated.
256 devices in a mesh: batch: 4 (over y), frame: 4 (over x_hi, core), space: 16 (over x_lo, z).
Axes of the slice: x: 4 (x_hi: 2, x_lo: 2; x = x_hi * 2 + x_lo), y: 4, z: 8, core: 2. Of those that a mesh axis runs over, the one named last changes fastest.
Arguments:
- queries: bfloat16 [32, 16, 8, 8, 1536], P(('batch', 'frame'), 'space'), parts along dimension 0, may hold values from -6 to 6
- keys: bfloat16 [32, 16, 8, 8, 1536], P(('batch', 'frame'), 'space'), parts along dimension 0, may hold values from -6 to 6
- values: bfloat16 [32, 16, 8, 8, 1536], P(('batch', 'frame'), 'space'), parts along dimension 0, may hold values from -6 to 6
- hidden: bfloat16 [32, 16, 8, 8, 3072], P(('batch', 'frame'), 'space'), parts along dimension 0, may hold values from -6 to 6
- control: bfloat16 [32, 16, 8, 8, 3072], P(('batch', 'frame'), 'space'), parts along dimension 0, may hold values from -4 to 4
- gate: bfloat16 [3072], replicated, may hold values from 0.5 to 3
- out_weight: bfloat16 [1536, 3072], P(('frame', 'space')), may hold values from -0.15625 to 0.15625
Outputs:
- output: bfloat16 [32, 16, 8, 8, 3072], P(('batch', 'frame'), 'space'), parts along dimension 0
There are 4 independent parts, one for each index of `batch`. A program takes and returns all parts, laid end to end along the dimension named above; an argument that names none is the same for every part. Nothing has to cross between parts.
All inputs are finite; a program needn't handle non-finite values.
Results may differ from a plain program's by a relative error of at most 0.0034.
Values may be sent and summed in bfloat16 or wider, within the bound.
A program may use at most 128 MiB of HBM per device.

v0:
```python
import jax
import jax.numpy as jnp
from jax import lax
from jax.sharding import PartitionSpec as P

HEAD_DIM = 128


def from_behind(value, axis, steps):
    count = lax.axis_size(axis)
    first, last = (max(0, -steps), min(count, count - steps))
    return lax.ppermute(value, axis, [(source, source + steps) for source in range(first, last)])


def padded(shard, sides, width):
    for axis, dim in sides:
        devices, length = (lax.axis_size(axis), shard.shape[dim])
        up = [(i, (i + 1) % devices) for i in range(devices - 1)]
        down = [(j, i) for i, j in up]
        last = lax.slice_in_dim(shard, length - width, length, axis=dim)
        first = lax.slice_in_dim(shard, 0, width, axis=dim)
        before = lax.ppermute(last, axis, up)
        after = lax.ppermute(first, axis, down)
        shard = jnp.concatenate([before, shard, after], axis=dim)
    return shard


def spatial_block(framed, grid_cols):
    grid_rows_list = []
    for step_h in (-1, 0, 1):
        row_list = []
        for step_w in (-1, 0, 1):
            if step_h == 0 and step_w == 0:
                row_list.append(framed)
            else:
                row_list.append(from_behind(framed, "space", -(step_h * grid_cols + step_w)))
        grid_rows_list.append(jnp.stack(row_list, axis=3))
    return jnp.stack(grid_rows_list, axis=3)


def per_device(queries, keys, values, hidden, control, gate, out_weight):
    tile_frames, box_count, tile_size, unused_size, channels = queries.shape
    head_count = channels // HEAD_DIM
    score_scale = HEAD_DIM ** (-0.5)
    frame_count = lax.axis_size("frame")
    space_count = lax.axis_size("space")
    grid_cols = min(4, space_count)
    grid_rows = space_count // grid_cols
    frame_here = lax.axis_index("frame")
    space_here = lax.axis_index("space")
    row_here = space_here // grid_cols
    col_here = space_here % grid_cols
    stacked = jnp.stack([keys, values]).reshape(2, 1, tile_frames, tile_size, tile_size, channels)
    local_block = spatial_block(stacked, grid_cols)
    block = padded(local_block, (("frame", 1),), 1)
    key_rows = block[0].reshape(-1, channels)
    value_rows = block[1].reshape(-1, channels)
    steps_three = jnp.arange(3) - 1
    frame_ok = (frame_here + steps_three >= 0) & (frame_here + steps_three < frame_count)
    height_ok = (row_here + steps_three >= 0) & (row_here + steps_three < grid_rows)
    width_ok = (col_here + steps_three >= 0) & (col_here + steps_three < grid_cols)
    grid_live = (
        frame_ok[:, None, None, None, None, None]
        & height_ok[None, None, :, None, None, None]
        & width_ok[None, None, None, :, None, None]
    )
    live_keys = jnp.broadcast_to(grid_live, (3, tile_frames, 3, 3, tile_size, tile_size)).reshape(
        -1
    )
    allowed = live_keys[None, :]
    query_rows = queries.reshape(-1, channels)

    def one_head(head_number):
        first_col = head_number * HEAD_DIM
        head_queries = lax.dynamic_slice_in_dim(query_rows, first_col, HEAD_DIM, 1)
        head_keys = lax.dynamic_slice_in_dim(key_rows, first_col, HEAD_DIM, 1)
        head_values = lax.dynamic_slice_in_dim(value_rows, first_col, HEAD_DIM, 1)
        scores = jnp.einsum(
            "qe,ke->qk", head_queries, head_keys, preferred_element_type=jnp.float32
        )
        masked = jnp.where(allowed, scores * score_scale, -1e30)
        row_max = jnp.max(masked, axis=1, keepdims=True)
        weights = jnp.where(allowed, jnp.exp(masked - row_max), 0.0)
        row_total = jnp.sum(weights, axis=1, keepdims=True)
        blended = jnp.dot(
            weights.astype(jnp.bfloat16), head_values, preferred_element_type=jnp.float32
        )
        return (blended / row_total).astype(jnp.bfloat16)

    per_head = lax.map(one_head, jnp.arange(head_count, dtype=jnp.int32))
    attention = jnp.transpose(per_head, (1, 0, 2)).reshape(-1, channels)
    projected = jnp.dot(
        attention,
        lax.all_gather(out_weight, ("frame", "space"), axis=0, tiled=True),
        preferred_element_type=jnp.float32,
    )
    model_width = out_weight.shape[1]
    result = (
        hidden.reshape(-1, model_width).astype(jnp.float32)
        + gate.astype(jnp.float32)[None, :] * projected
    )
    result = result + control.reshape(-1, model_width).astype(jnp.float32)
    return result.astype(jnp.bfloat16).reshape(hidden.shape)


def solution(mesh):
    return jax.shard_map(
        per_device,
        mesh=mesh,
        in_specs=(
            P(("batch", "frame"), "space", None, None, None),
            P(("batch", "frame"), "space", None, None, None),
            P(("batch", "frame"), "space", None, None, None),
            P(("batch", "frame"), "space", None, None, None),
            P(("batch", "frame"), "space", None, None, None),
            P(),
            P(("frame", "space"), None),
        ),
        out_specs=P(("batch", "frame"), "space", None, None, None),
        check_vma=False,
    )
```

profile of v0, /device:TPU:123, one launch (start us, length us, event | category | flops | bytes accessed | tf_op | source)
XLA Modules:
  0.0 495.2 jit_solution(3634493028845217952)
XLA Ops:
  9.1 6.1 %collective-permute-start.1 = (bf16[2,1,2,8,8,1536]{5,4,3,2,0,1:T(8,128)(2,1)S(1)}, bf16[2,1,2,8,8,1536]{5,4,3,2,0,1:T(8,128)(2,1)S(1)}, u32[]{:S(2)}, u32[]{:S(2)}) collective-permute-start(bf16[2,1,2,8,8,1536]{5,4,3,2,0,1:T(8,128)(2,1)S(1)} %get-tuple-element.79), channel_id=1, source_target_pairs={{0,4},{1,5},{2,6},{3,7},{4,8},{5,9},{6,10},{7,11},{8,12},{9,13},{1... | collective-permute-start | bytes 2359304 | tf_op jit(solution)/shard_map/ppermute | solution.py:12
  15.2 1.9 collective-permute-start.2
  17.1 5.2 %collective-permute-start.5 = (bf16[2,1,2,8,8,1536]{5,4,3,2,0,1:T(8,128)(2,1)S(1)}, bf16[2,1,2,8,8,1536]{5,4,3,2,0,1:T(8,128)(2,1)S(1)}, u32[]{:S(2)}, u32[]{:S(2)}) collective-permute-start(bf16[2,1,2,8,8,1536]{5,4,3,2,0,1:T(8,128)(2,1)S(1)} %get-tuple-element.79), channel_id=1, source_target_pairs={{3,0},{4,1},{5,2},{6,3},{7,4},{8,5},{9,6},{10,7},{11,8},{12,9},{13... | collective-permute-start | bytes 2359304 | tf_op jit(solution)/shard_map/ppermute | solution.py:12
  22.3 6.7 %collective-permute-start.6 = (bf16[2,1,2,8,8,1536]{5,4,3,2,0,1:T(8,128)(2,1)S(1)}, bf16[2,1,2,8,8,1536]{5,4,3,2,0,1:T(8,128)(2,1)S(1)}, u32[]{:S(2)}, u32[]{:S(2)}) collective-permute-start(bf16[2,1,2,8,8,1536]{5,4,3,2,0,1:T(8,128)(2,1)S(1)} %get-tuple-element.79), channel_id=1, source_target_pairs={{4,0},{5,1},{6,2},{7,3},{8,4},{9,5},{10,6},{11,7},{12,8},{13,9},{1... | collective-permute-start | bytes 2359304 | tf_op jit(solution)/shard_map/ppermute | solution.py:12
  29.0 33.4 %collective-permute-done = bf16[2,1,2,8,8,1536]{5,4,3,2,0,1:T(8,128)(2,1)S(1)} collective-permute-done((bf16[2,1,2,8,8,1536]{5,4,3,2,0,1:T(8,128)(2,1)S(1)}, bf16[2,1,2,8,8,1536]{5,4,3,2,0,1:T(8,128)(2,1)S(1)}, u32[]{:S(2)}, u32[]{:S(2)}) %collective-permute-start) | collective-permute-done | bytes 786464 | tf_op jit(solution)/shard_map/ppermute | solution.py:12
  62.4 5.0 %collective-permute-start.7 = (bf16[2,1,2,8,8,1536]{5,4,3,2,0,1:T(8,128)(2,1)S(1)}, bf16[2,1,2,8,8,1536]{5,4,3,2,0,1:T(8,128)(2,1)S(1)}, u32[]{:S(2)}, u32[]{:S(2)}) collective-permute-start(bf16[2,1,2,8,8,1536]{5,4,3,2,0,1:T(8,128)(2,1)S(1)} %get-tuple-element.79), channel_id=1, source_target_pairs={{5,0},{6,1},{7,2},{8,3},{9,4},{10,5},{11,6},{12,7},{13,8},{14,9},{... | collective-permute-start | bytes 2359304 | tf_op jit(solution)/shard_map/ppermute | solution.py:12
  67.4 19.6 %collective-permute-done.1 = bf16[2,1,2,8,8,1536]{5,4,3,2,0,1:T(8,128)(2,1)S(1)} collective-permute-done((bf16[2,1,2,8,8,1536]{5,4,3,2,0,1:T(8,128)(2,1)S(1)}, bf16[2,1,2,8,8,1536]{5,4,3,2,0,1:T(8,128)(2,1)S(1)}, u32[]{:S(2)}, u32[]{:S(2)}) %collective-permute-start.1) | collective-permute-done | bytes 786464 | tf_op jit(solution)/shard_map/ppermute | solution.py:12
  87.0 8.5 %collective-permute-start.4 = (bf16[2,1,2,8,8,1536]{5,4,3,2,0,1:T(8,128)(2,1)S(1)}, bf16[2,1,2,8,8,1536]{5,4,3,2,0,1:T(8,128)(2,1)S(1)}, u32[]{:S(2)}, u32[]{:S(2)}) collective-permute-start(bf16[2,1,2,8,8,1536]{5,4,3,2,0,1:T(8,128)(2,1)S(1)} %get-tuple-element.79), channel_id=1, source_target_pairs={{1,0},{2,1},{3,2},{4,3},{5,4},{6,5},{7,6},{8,7},{9,8},{10,9},{11,1... | collective-permute-start | bytes 2359304 | tf_op jit(solution)/shard_map/ppermute | solution.py:12
  95.5 45.0 %collective-permute-start.3 = (bf16[2,1,2,8,8,1536]{5,4,3,2,0,1:T(8,128)(2,1)S(1)}, bf16[2,1,2,8,8,1536]{5,4,3,2,0,1:T(8,128)(2,1)S(1)}, u32[]{:S(2)}, u32[]{:S(2)}) collective-permute-start(bf16[2,1,2,8,8,1536]{5,4,3,2,0,1:T(8,128)(2,1)S(1)} %get-tuple-element.79), channel_id=1, source_target_pairs={{0,1},{1,2},{2,3},{3,4},{4,5},{5,6},{6,7},{7,8},{8,9},{9,10},{10,1... | collective-permute-start | bytes 2359304 | tf_op jit(solution)/shard_map/ppermute | solution.py:12
  141.1 80.8 %collective-permute-done.3 = bf16[2,1,2,8,8,1536]{5,4,3,2,0,1:T(8,128)(2,1)S(1)} collective-permute-done((bf16[2,1,2,8,8,1536]{5,4,3,2,0,1:T(8,128)(2,1)S(1)}, bf16[2,1,2,8,8,1536]{5,4,3,2,0,1:T(8,128)(2,1)S(1)}, u32[]{:S(2)}, u32[]{:S(2)}) %collective-permute-start.3) | collective-permute-done | bytes 786464 | tf_op jit(solution)/shard_map/ppermute | solution.py:12
  222.2 3.7 pad_maximum_fusion.1
  225.9 5.0 %collective-permute-start.8 = (bf16[2,1,2,3,3,8,8,1536]{7,6,5,2,0,4,3,1:T(8,128)(2,1)}, bf16[2,1,2,3,3,8,8,1536]{7,6,5,2,0,4,3,1:T(8,128)(2,1)}, u32[]{:S(2)}, u32[]{:S(2)}) collective-permute-start(bf16[2,1,2,3,3,8,8,1536]{7,6,5,2,0,4,3,1:T(8,128)(2,1)} %pad_maximum_fusion.1), channel_id=1, source_target_pairs={{0,16},{16,32},{32,48},{1,17},{17,33},{33,49},{2,18},{18,34},{34,5... | collective-permute-start | bytes 21233672 | tf_op jit(solution)/shard_map/ppermute | solution.py:22
  230.9 2.5 collective-permute-start.9
  233.7 73.9 %collective-permute-done.8 = bf16[2,1,2,3,3,8,8,1536]{7,6,5,2,0,4,3,1:T(8,128)(2,1)} collective-permute-done((bf16[2,1,2,3,3,8,8,1536]{7,6,5,2,0,4,3,1:T(8,128)(2,1)}, bf16[2,1,2,3,3,8,8,1536]{7,6,5,2,0,4,3,1:T(8,128)(2,1)}, u32[]{:S(2)}, u32[]{:S(2)}) %collective-permute-start.8) | collective-permute-done | bytes 7077920 | tf_op jit(solution)/shard_map/ppermute | solution.py:22
  307.5 13.8 %collective-permute-done.9 = bf16[2,1,2,3,3,8,8,1536]{7,6,5,2,0,4,3,1:T(8,128)(2,1)} collective-permute-done((bf16[2,1,2,3,3,8,8,1536]{7,6,5,2,0,4,3,1:T(8,128)(2,1)}, bf16[2,1,2,3,3,8,8,1536]{7,6,5,2,0,4,3,1:T(8,128)(2,1)}, u32[]{:S(2)}, u32[]{:S(2)}) %collective-permute-start.9) | collective-permute-done | bytes 7077920 | tf_op jit(solution)/shard_map/ppermute | solution.py:23
  321.3 8.0 %pad_maximum_fusion = bf16[2,3,2,3,3,8,8,1536]{7,6,5,2,0,4,3,1:T(8,128)(2,1)S(1)} fusion(bf16[2,1,2,3,3,8,8,1536]{7,6,5,2,0,4,3,1:T(8,128)(2,1)} %collective-permute-done.9, bf16[2,1,2,1,3,8,8,1536]{7,6,5,2,0,4,3,1:T(8,128)(2,1)} %copy-done, bf16[2,1,2,1,3,8,8,1536]{7,6,5,2,0,4,3,1:T(8,128)(2,1)} %copy-done.1, ...), kind=kLoop, calls=%fused_computation.19 | loop fusion | flops 42467328 | bytes 42467328 | tf_op jit(solution)/shard_map/concatenate | solution.py:24
  329.4 5.3 %fusion.23 = (bf16[1,3,2,3,3,8,8,1536]{7,6,5,2,0,4,3,1:T(8,128)(2,1)S(1)}, bf16[1,3,2,3,3,8,8,1536]{7,6,5,2,0,4,3,1:T(8,128)(2,1)}) fusion(bf16[2,3,2,3,3,8,8,1536]{7,6,5,2,0,4,3,1:T(8,128)(2,1)S(1)} %pad_maximum_fusion), kind=kLoop, calls=%fused_computation.38 | loop fusion | bytes 42467328 | tf_op jit(solution)/shard_map/slice | solution.py:57
  334.7 9.4 %copy.11 = bf16[1,3,2,3,3,8,8,1536]{7,6,5,4,3,2,1,0:T(8,128)(2,1)} copy(bf16[1,3,2,3,3,8,8,1536]{7,6,5,2,0,4,3,1:T(8,128)(2,1)} %get-tuple-element.77) | data formatting | bytes 21233664 | tf_op jit(solution)/shard_map/slice | solution.py:56
  344.1 4.6 copy.12
  348.7 66.1 %while.11 = (s32[]{:T(128)}, bf16[12,128,128]{1,2,0:T(8,128)(2,1)S(1)}, s32[12]{0:T(128)S(1)}, bf16[128,1536]{1,0:T(8,128)(2,1)}, bf16[3456,1536]{1,0:T(8,128)(2...) while((s32[]{:T(128)}, ...), condition=%wide.region_3.4_spmd.clone, body=%wide.region_0.3_spmd.clone.sunk | while | flops 230506240 | bytes 7299018 | solution.py:90
  350.3 1.7 fusion.33
  388.8 1.7 fusion.33
  414.8 67.2 %all-gather.2.cloned.1.call-done = bf16[1536,3072]{1,0:T(8,128)(2,1)} async-done(((bf16[24,3072]{1,0:T(8,128)(2,1)}), bf16[1536,3072]{1,0:T(8,128)(2,1)}) %all-gather.2.cloned.1.call-update) | async-done | bytes 9437200 | tf_op jit(solution)/shard_map/all_gather | solution.py:94
  482.0 6.3 %fusion.19 = bf16[128,3072]{1,0:T(8,128)(2,1)} fusion(bf16[128,1536]{0,1:T(8,128)(2,1)S(1)} %bitcast.46, bf16[1536,3072]{1,0:T(8,128)(2,1)} %all-gather.2.cloned.1.call-done, bf16[128,3072]{1,0:T(8,128)(2,1)S(1)} %bitcast.47, bf16[128,3072]{1,0:T(8,128)(2,1)S(1)} %bitcast.48, f32[3072]{0:T(1024)S(1)} %convert_element_type.26), kind=kOutput, calls=%fused_computation.24 | convolution fusion | flops 1210318848 | bytes 12201984 | tf_op jit(solution)/shard_map/dot_general | solution.py:92
  (123 shorter events, 58.1 us)
Async XLA Ops:
  6.5 475.5 %all-gather.2.cloned.1.call-start = ((), (), s32[]{:S(2)}) async-start(), calls=%async_computation | async-start | bytes 9584640 | tf_op jit(solution)/shard_map/all_gather | solution.py:94
  7.8 54.7 %collective-permute-start = (bf16[2,1,2,8,8,1536]{5,4,3,2,0,1:T(8,128)(2,1)S(1)}, bf16[2,1,2,8,8,1536]{5,4,3,2,0,1:T(8,128)(2,1)S(1)}, u32[]{:S(2)}, u32[]{:S(2)}) collective-permute-start(bf16[2,1,2,8,8,1536]{5,4,3,2,0,1:T(8,128)(2,1)S(1)} %get-tuple-element.79), channel_id=1, source_target_pairs={{0,5},{1,6},{2,7},{3,8},{4,9},{5,10},{6,11},{7,12},{8,13},{9,14},{... | collective-permute-start | bytes 2359304 | tf_op jit(solution)/shard_map/ppermute | solution.py:12
  9.1 78.0 %collective-permute-start.1 = (bf16[2,1,2,8,8,1536]{5,4,3,2,0,1:T(8,128)(2,1)S(1)}, bf16[2,1,2,8,8,1536]{5,4,3,2,0,1:T(8,128)(2,1)S(1)}, u32[]{:S(2)}, u32[]{:S(2)}) collective-permute-start(bf16[2,1,2,8,8,1536]{5,4,3,2,0,1:T(8,128)(2,1)S(1)} %get-tuple-element.79), channel_id=1, source_target_pairs={{0,4},{1,5},{2,6},{3,7},{4,8},{5,9},{6,10},{7,11},{8,12},{9,13},{1... | collective-permute-start | bytes 2359304 | tf_op jit(solution)/shard_map/ppermute | solution.py:12
  15.2 80.3 %collective-permute-start.2 = (bf16[2,1,2,8,8,1536]{5,4,3,2,0,1:T(8,128)(2,1)S(1)}, bf16[2,1,2,8,8,1536]{5,4,3,2,0,1:T(8,128)(2,1)S(1)}, u32[]{:S(2)}, u32[]{:S(2)}) collective-permute-start(bf16[2,1,2,8,8,1536]{5,4,3,2,0,1:T(8,128)(2,1)S(1)} %get-tuple-element.79), channel_id=1, source_target_pairs={{0,3},{1,4},{2,5},{3,6},{4,7},{5,8},{6,9},{7,10},{8,11},{9,12},{10... | collective-permute-start | bytes 2359304 | tf_op jit(solution)/shard_map/ppermute | solution.py:12
  17.1 123.7 %collective-permute-start.5 = (bf16[2,1,2,8,8,1536]{5,4,3,2,0,1:T(8,128)(2,1)S(1)}, bf16[2,1,2,8,8,1536]{5,4,3,2,0,1:T(8,128)(2,1)S(1)}, u32[]{:S(2)}, u32[]{:S(2)}) collective-permute-start(bf16[2,1,2,8,8,1536]{5,4,3,2,0,1:T(8,128)(2,1)S(1)} %get-tuple-element.79), channel_id=1, source_target_pairs={{3,0},{4,1},{5,2},{6,3},{7,4},{8,5},{9,6},{10,7},{11,8},{12,9},{13... | collective-permute-start | bytes 2359304 | tf_op jit(solution)/shard_map/ppermute | solution.py:12
  22.3 118.5 %collective-permute-start.6 = (bf16[2,1,2,8,8,1536]{5,4,3,2,0,1:T(8,128)(2,1)S(1)}, bf16[2,1,2,8,8,1536]{5,4,3,2,0,1:T(8,128)(2,1)S(1)}, u32[]{:S(2)}, u32[]{:S(2)}) collective-permute-start(bf16[2,1,2,8,8,1536]{5,4,3,2,0,1:T(8,128)(2,1)S(1)} %get-tuple-element.79), channel_id=1, source_target_pairs={{4,0},{5,1},{6,2},{7,3},{8,4},{9,5},{10,6},{11,7},{12,8},{13,9},{1... | collective-permute-start | bytes 2359304 | tf_op jit(solution)/shard_map/ppermute | solution.py:12
  62.4 78.4 %collective-permute-start.7 = (bf16[2,1,2,8,8,1536]{5,4,3,2,0,1:T(8,128)(2,1)S(1)}, bf16[2,1,2,8,8,1536]{5,4,3,2,0,1:T(8,128)(2,1)S(1)}, u32[]{:S(2)}, u32[]{:S(2)}) collective-permute-start(bf16[2,1,2,8,8,1536]{5,4,3,2,0,1:T(8,128)(2,1)S(1)} %get-tuple-element.79), channel_id=1, source_target_pairs={{5,0},{6,1},{7,2},{8,3},{9,4},{10,5},{11,6},{12,7},{13,8},{14,9},{... | collective-permute-start | bytes 2359304 | tf_op jit(solution)/shard_map/ppermute | solution.py:12
  87.0 54.1 %collective-permute-start.4 = (bf16[2,1,2,8,8,1536]{5,4,3,2,0,1:T(8,128)(2,1)S(1)}, bf16[2,1,2,8,8,1536]{5,4,3,2,0,1:T(8,128)(2,1)S(1)}, u32[]{:S(2)}, u32[]{:S(2)}) collective-permute-start(bf16[2,1,2,8,8,1536]{5,4,3,2,0,1:T(8,128)(2,1)S(1)} %get-tuple-element.79), channel_id=1, source_target_pairs={{1,0},{2,1},{3,2},{4,3},{5,4},{6,5},{7,6},{8,7},{9,8},{10,9},{11,1... | collective-permute-start | bytes 2359304 | tf_op jit(solution)/shard_map/ppermute | solution.py:12
  95.5 126.4 %collective-permute-start.3 = (bf16[2,1,2,8,8,1536]{5,4,3,2,0,1:T(8,128)(2,1)S(1)}, bf16[2,1,2,8,8,1536]{5,4,3,2,0,1:T(8,128)(2,1)S(1)}, u32[]{:S(2)}, u32[]{:S(2)}) collective-permute-start(bf16[2,1,2,8,8,1536]{5,4,3,2,0,1:T(8,128)(2,1)S(1)} %get-tuple-element.79), channel_id=1, source_target_pairs={{0,1},{1,2},{2,3},{3,4},{4,5},{5,6},{6,7},{7,8},{8,9},{9,10},{10,1... | collective-permute-start | bytes 2359304 | tf_op jit(solution)/shard_map/ppermute | solution.py:12
  141.1 81.1 %copy-start = (bf16[2,1,2,1,3,8,8,1536]{7,6,5,2,0,4,3,1:T(8,128)(2,1)}, bf16[2,1,2,1,3,8,8,1536]{7,6,5,2,0,4,3,1:T(8,128)(2,1)S(1)}, u32[]{:S(2)}) copy-start(bf16[2,1,2,1,3,8,8,1536]{7,6,5,2,0,4,3,1:T(8,128)(2,1)S(1)} %maximum_bitcast_fusion.2) | copy-start | bytes 7077892
  222.2 3.7 copy-start.1
  222.2 11.3 %copy-start.4 = (bf16[3072]{0:T(1024)(128)(2,1)S(1)}, bf16[3072]{0:T(1024)(128)(2,1)}, u32[]{:S(2)}) copy-start(bf16[3072]{0:T(1024)(128)(2,1)} %param.14) | copy-start | bytes 18436
  225.9 81.7 %collective-permute-start.8 = (bf16[2,1,2,3,3,8,8,1536]{7,6,5,2,0,4,3,1:T(8,128)(2,1)}, bf16[2,1,2,3,3,8,8,1536]{7,6,5,2,0,4,3,1:T(8,128)(2,1)}, u32[]{:S(2)}, u32[]{:S(2)}) collective-permute-start(bf16[2,1,2,3,3,8,8,1536]{7,6,5,2,0,4,3,1:T(8,128)(2,1)} %pad_maximum_fusion.1), channel_id=1, source_target_pairs={{0,16},{16,32},{32,48},{1,17},{17,33},{33,49},{2,18},{18,34},{34,5... | collective-permute-start | bytes 21233672 | tf_op jit(solution)/shard_map/ppermute | solution.py:22
  230.9 90.4 %collective-permute-start.9 = (bf16[2,1,2,3,3,8,8,1536]{7,6,5,2,0,4,3,1:T(8,128)(2,1)}, bf16[2,1,2,3,3,8,8,1536]{7,6,5,2,0,4,3,1:T(8,128)(2,1)}, u32[]{:S(2)}, u32[]{:S(2)}) collective-permute-start(bf16[2,1,2,3,3,8,8,1536]{7,6,5,2,0,4,3,1:T(8,128)(2,1)} %pad_maximum_fusion.1), channel_id=1, source_target_pairs={{16,0},{32,16},{48,32},{17,1},{33,17},{49,33},{18,2},{34,18},{50,3... | collective-permute-start | bytes 21233672 | tf_op jit(solution)/shard_map/ppermute | solution.py:23
  348.7 133.3 %copy-start.2 = (bf16[2,1,8,8,3072]{4,3,2,1,0:T(8,128)(2,1)S(1)}, bf16[2,1,8,8,3072]{4,3,2,1,0:T(8,128)(2,1)}, u32[]{:S(2)}) copy-start(bf16[2,1,8,8,3072]{4,3,2,1,0:T(8,128)(2,1)} %param.13) | copy-start | bytes 2359300
  348.7 133.3 %copy-start.3 = (bf16[2,1,8,8,3072]{4,3,2,1,0:T(8,128)(2,1)S(1)}, bf16[2,1,8,8,3072]{4,3,2,1,0:T(8,128)(2,1)}, u32[]{:S(2)}) copy-start(bf16[2,1,8,8,3072]{4,3,2,1,0:T(8,128)(2,1)} %param.12) | copy-start | bytes 2359300
Sparse Core Ops, SparseCore 0:
  233.5 248.4 all-gather.1
where the time goes:
time: 497 us; the launch traced here: 495 us
  waiting for transfers between devices  289 us (58%)
  starting transfers between devices  87.2 us (18%)
  matrix products  46.3 us (9%)
  local copies, waits for them, and re-layouts  31.7 us (6%)
  other arithmetic  19.5 us (4%)
  between operations  13.7 us (3%)
  loops' own time  8.13 us (2%)
    ppermute x8, waiting for transfers between devices, from_behind(): lax.ppermute(value, axis, [(source, source + steps) for source in range(f...  134 us
    ppermute x8, starting transfers between devices, from_behind(): lax.ppermute(value, axis, [(source, source + steps) for source in range(f...  79.7 us
    ppermute x1, waiting for transfers between devices, padded(): before = lax.ppermute(last, axis, up)  73.9 us
    all_gather x1, waiting for transfers between devices, per_device(): lax.all_gather(out_weight, ('frame', 'space'), axis=0, tiled=True)  67.2 us
    dot_general x12, matrix products, one_head(): jnp.einsum('qe,ke->qk', head_queries, head_keys, preferred_element_type=j...  20.2 us
    dot_general x12, matrix products, one_head(): jnp.dot(weights.astype(jnp.bfloat16), head_values, preferred_element_type...  19.8 us
    ppermute x1, waiting for transfers between devices, padded(): after = lax.ppermute(first, axis, down)  13.8 us
    slice x2, local copies, waits for them, and re-layouts, per_device(): value_rows = block[1].reshape(-1, channels)  9.95 us
  transfers between devices with their start and end apart: 11, of which 6 were waited for; matrix products, arithmetic and copies ran while one was open for 17% of the time, Pallas kernels for 0%

commit v1 on v0

v1 whole, which is shorter than its diff:
```python
import functools

import jax
import jax.numpy as jnp
from jax import lax
from jax.experimental import pallas as pl
from jax.experimental.pallas import tpu as pltpu
from jax.sharding import PartitionSpec as P

HD = 128
ROWS = 128
NH = 12
NB = 16
GW = 4
NY = 4
NF = 4
NZ = 8
MESH = pl.DeviceIdType.MESH
SCALE = HD ** -0.5 * 1.4426950408889634


def window(box):
    r, c = box // GW, box % GW
    return range(max(r - 1, 0), min(r + 2, GW)), max(c - 1, 0), min(c + 2, GW)


def kernel(q_hbm, k_hbm, v_hbm, w_hbm, attn, wfull,
           qbuf, kbuf, vbuf, obuf, mbuf, lbuf, acc,
           s_snd, k_rcv, v_rcv, q_rcv, h_snd, h_rcv, o_snd, o_rcv,
           w1s, w1r, w2s, w2r, w3s, w3r, w4s, w4r, w5s, w5r):
    y, f, s = lax.axis_index("batch"), lax.axis_index("frame"), lax.axis_index("space")
    lo, z = s // NZ, s % NZ
    hi, core = f // 2, f % 2
    quarter = wfull.shape[-1] // NY
    owner = s % 4 != 3
    my_head = (s // 4) * 3 + s % 4
    partner = f + 1 - 2 * core
    cross = f - 1 + 2 * core
    has_cross = (f == 1) | (f == 2)
    x = hi * 2 + lo
    xr, xl = (x + 1) % 4, (x + 3) % 4
    yr, yl = (y + 1) % NY, (y + NY - 1) % NY

    def at_x(pos):
        return (y, (pos // 2) * 2 + core, (pos % 2) * NZ + z)

    def wcols(yy):
        return pl.ds(pl.multiple_of(yy * quarter, 128), quarter)

    barrier = pltpu.get_barrier_semaphore()

    def greet(i, carry):
        pl.semaphore_signal(barrier, inc=1, device_id=(y, f, (s + i) % NB), device_id_type=MESH)
        return carry

    lax.fori_loop(1, NB, greet, 0)
    other_f = (f + 2) % NF
    for dev in ((y, other_f, s), (y, other_f, (s + NZ) % NB), (yr, f, s), (yl, f, s), (y, partner, s)):
        pl.semaphore_signal(barrier, inc=1, device_id=dev, device_id_type=MESH)

    @pl.when(has_cross)
    def _():
        pl.semaphore_signal(barrier, inc=1, device_id=(y, cross, s), device_id_type=MESH)

    pl.semaphore_wait(barrier, jnp.where(has_cross, NB + 5, NB + 4))

    def remote(src, dst, snd, rcv, dev):
        return pltpu.make_async_remote_copy(
            src_ref=src, dst_ref=dst, send_sem=snd, recv_sem=rcv, device_id=dev, device_id_type=MESH)

    def await_copy(ref, sem):
        pltpu.make_async_copy(ref, ref, sem).wait()

    def w1(i):
        zz = (z + i) % NZ
        return remote(w_hbm.at[:, wcols(y)], wfull.at[f, s, :, wcols(y)], w1s.at[zz], w1r.at[z],
                      (y, f, lo * NZ + zz))

    def start_w1(i, carry):
        w1(i).start()
        return carry

    pltpu.make_async_copy(w_hbm.at[:, wcols(y)], wfull.at[f, s, :, wcols(y)], w1r.at[z]).start()
    lax.fori_loop(1, NZ, start_w1, 0)

    first = (s // 4) * 3 + jnp.minimum(s % 4, 2)

    def head_of(i):
        h = (first + i) % NH
        return h, (h // 3) * 4 + h % 3

    def piece(ref, h):
        return ref.at[:, pl.ds(pl.multiple_of(h * HD, HD), HD)]

    streams = ((0, k_hbm, kbuf.at[0], k_rcv), (1, v_hbm, vbuf.at[0], v_rcv), (2, q_hbm, qbuf, q_rcv))

    def send_heads(which):
        def step(i, carry):
            h, to = head_of(i)
            for n in which:
                row, src, dst, rcv = streams[n]

                @pl.when(to == s)
                def _():
                    pltpu.make_async_copy(piece(src, h), dst.at[s], rcv.at[s]).start()

                @pl.when(to != s)
                def _():
                    remote(piece(src, h), dst.at[s], s_snd.at[row, h], rcv.at[s], (y, f, to)).start()
            return carry

        lax.fori_loop(0, NH, step, 0)

    send_heads((0, 1))
    send_heads((2,))

    def await_w1(i, carry):
        await_copy(wfull.at[f, lo * NZ + i, :, wcols(y)], w1r.at[i])
        return carry

    lax.fori_loop(0, NZ, await_w1, 0)

    def xblock(pos, start=0, count=NZ):
        return wfull.at[(pos // 2) * 2 + core, pl.ds((pos % 2) * NZ + start, count), :, wcols(y)]

    own_r = remote(xblock(x), xblock(x), w2s.at[0], w2r.at[0], at_x(xr))
    own_l = remote(xblock(x), xblock(x), w2s.at[1], w2r.at[1], at_x(xl))
    rel_r = remote(xblock(xl, 0, 4), xblock(xl, 0, 4), w2s.at[2], w2r.at[2], at_x(xr))
    rel_l = remote(xblock(xr, 4, 4), xblock(xr, 4, 4), w2s.at[3], w2r.at[3], at_x(xl))
    own_r.start()
    own_l.start()

    def forward(i):
        box = (s + NB - i) % NB
        out = []
        for n, (buf, rcv) in enumerate(((kbuf, k_rcv), (vbuf, v_rcv))):
            out.append((buf, rcv, box,
                        remote(buf.at[0, box], buf.at[1, box], h_snd.at[n, 0, box], h_rcv.at[n, 0, box],
                               (y, partner, s)),
                        remote(buf.at[0, box], buf.at[2, box], h_snd.at[n, 1, box], h_rcv.at[n, 1, box],
                               (y, cross, s))))
        return out

    def forward_step(i, carry):
        for buf, rcv, box, near, far in forward(i):
            await_copy(buf.at[0, box], rcv.at[box])

            @pl.when(has_cross)
            def _():
                far.start()

            near.start()
        return carry

    @pl.when(owner)
    def _():
        mbuf[...] = jnp.full_like(mbuf, -1e30)
        lbuf[...] = jnp.zeros_like(lbuf)
        acc[...] = jnp.zeros_like(acc)
        lax.fori_loop(0, 8, forward_step, 0)

    await_copy(xblock(xl), w2r.at[0])
    await_copy(xblock(xr), w2r.at[1])
    rel_r.start()
    rel_l.start()

    @pl.when(owner)
    def _():
        lax.fori_loop(8, NB, forward_step, 0)

    x2 = (x + 2) % 4
    await_copy(xblock(x2, 0, 4), w2r.at[2])
    await_copy(xblock(x2, 4, 4), w2r.at[3])

    def wblock(yy, n, side):
        return wfull.at[side + 2 * n, :, :, wcols(yy)]

    y2 = (y + 2) % NY

    def to_partner(n, m):
        yy = (y, yl, yr, y2)[n]
        return remote(wblock(yy, m, core), wblock(yy, m, core), w5s.at[2 * n + m], w5r.at[2 * n + m],
                      (y, partner, s))

    def y_own(d, m):
        return remote(wblock(y, m, core), wblock(y, m, core), w3s.at[2 * d + m], w3r.at[2 * d + m],
                      ((yr, yl)[d], f, s))

    y_rel = (remote(wblock(yl, 0, core), wblock(yl, 0, core), w4s.at[0], w4r.at[0], (yr, f, s)),
             remote(wblock(yr, 1, core), wblock(yr, 1, core), w4s.at[1], w4r.at[1], (yl, f, s)))
    for d, m in ((0, 0), (1, 1), (0, 1), (1, 0)):
        y_own(d, m).start()
    for m in (0, 1):
        to_partner(0, m).start()

    def relay_weight():
        await_copy(wblock(yl, 0, core), w3r.at[0])
        y_rel[0].start()
        await_copy(wblock(yr, 1, core), w3r.at[3])
        y_rel[1].start()
        to_partner(1, 0).start()
        to_partner(2, 1).start()
        await_copy(wblock(yl, 1, core), w3r.at[1])
        to_partner(1, 1).start()
        await_copy(wblock(yr, 0, core), w3r.at[2])
        to_partner(2, 0).start()

    frames = jnp.where(has_cross, 3, 2)

    def send_o(box, start):
        @pl.when(s == box)
        def _():
            if start:
                pltpu.make_async_copy(obuf.at[box], piece(attn, my_head), o_rcv.at[my_head]).start()

        @pl.when(s != box)
        def _():
            cp = remote(obuf.at[box], piece(attn, my_head), o_snd.at[box], o_rcv.at[my_head], (y, f, box))
            if start:
                cp.start()
            else:
                cp.wait_send()

    def one_frame(j, carry):
        @pl.when(j == 1)
        def _():
            relay_weight()

        for box in range(NB):
            rows, c0, c1 = window(box)
            if box % GW == 0:
                fresh = (0, 1) if box == 0 else ((box // GW + 1,) if box // GW + 1 < GW else ())

                @pl.when(j > 0)
                def _():
                    for r in fresh:
                        for b in range(r * GW, r * GW + GW):
                            await_copy(kbuf.at[j, b], h_rcv.at[0, j - 1, b])
                            await_copy(vbuf.at[j, b], h_rcv.at[1, j - 1, b])

            @pl.when(j == 0)
            def _():
                await_copy(qbuf.at[box], q_rcv.at[box])

            n = (c1 - c0) * ROWS
            q = qbuf[box]
            scores = [lax.dot_general(q, kbuf[j, r * GW + c0:r * GW + c1].reshape(n, HD),
                                      (((1,), (1,)), ((), ())), preferred_element_type=jnp.float32)
                      for r in rows]
            top = functools.reduce(jnp.maximum, scores)
            m_old = mbuf[box]
            m_new = jnp.maximum(m_old, jnp.max(top, axis=1, keepdims=True))
            alpha = jnp.exp2((m_old - m_new) * SCALE)
            shift = m_new[:, :1] * SCALE
            total = lbuf[box] * alpha
            out = acc[box] * alpha
            for r, sc in zip(rows, scores):
                p = jnp.exp2(sc * SCALE - shift)
                total = total + jnp.sum(p, axis=1, keepdims=True)
                out = out + jnp.dot(p.astype(jnp.bfloat16),
                                    vbuf[j, r * GW + c0:r * GW + c1].reshape(n, HD),
                                    preferred_element_type=jnp.float32)
            mbuf[box] = m_new
            lbuf[box] = total
            acc[box] = out

            @pl.when(j == frames - 1)
            def _():
                obuf[box] = (out / total).astype(jnp.bfloat16)
                if box:
                    send_o(box - 1, True)
        return carry

    @pl.when(owner)
    def _():
        lax.fori_loop(0, frames, one_frame, 0)
        send_o(NB - 1, True)

    @pl.when(jnp.logical_not(owner))
    def _():
        relay_weight()

    await_copy(wblock(y2, 0, core), w4r.at[0])
    to_partner(3, 0).start()
    await_copy(wblock(y2, 1, core), w4r.at[1])
    to_partner(3, 1).start()

    def await_o(h, carry):
        await_copy(piece(attn, h), o_rcv.at[h])
        return carry

    lax.fori_loop(0, NH, await_o, 0)
    for n in range(4):
        for m in (0, 1):
            await_copy(wblock((y, yl, yr, y2)[n], m, 1 - core), w5r.at[2 * n + m])

    def drain_heads(i, carry):
        h, to = head_of(i)

        @pl.when(to != s)
        def _():
            for row, src, dst, rcv in streams:
                remote(piece(src, h), dst.at[s], s_snd.at[row, h], rcv.at[s], (y, f, to)).wait_send()
        return carry

    lax.fori_loop(0, NH, drain_heads, 0)

    def drain_w1(i, carry):
        w1(i).wait_send()
        return carry

    lax.fori_loop(1, NZ, drain_w1, 0)
    for cp in (own_r, own_l, rel_r, rel_l) + y_rel:
        cp.wait_send()
    for d in (0, 1):
        for m in (0, 1):
            y_own(d, m).wait_send()
    for n in range(4):
        for m in (0, 1):
            to_partner(n, m).wait_send()

    @pl.when(owner)
    def _():
        def drain(i, carry):
            for _, _, _, near, far in forward(i):
                near.wait_send()

                @pl.when(has_cross)
                def _():
                    far.wait_send()
            return carry

        lax.fori_loop(0, NB, drain, 0)
        for box in range(NB):
            send_o(box, False)


def gather_and_attend(q, k, v, w):
    dma = pltpu.SemaphoreType.DMA
    any_spec = pl.BlockSpec(memory_space=pl.ANY)
    return pl.pallas_call(
        kernel,
        out_shape=(jax.ShapeDtypeStruct(q.shape, q.dtype),
                   jax.ShapeDtypeStruct((NF, NB) + w.shape, w.dtype)),
        in_specs=[any_spec] * 4,
        out_specs=(any_spec, any_spec),
        scratch_shapes=[
            pltpu.VMEM((NB, ROWS, HD), jnp.bfloat16),
            pltpu.VMEM((3, NB, ROWS, HD), jnp.bfloat16),
            pltpu.VMEM((3, NB, ROWS, HD), jnp.bfloat16),
            pltpu.VMEM((NB, ROWS, HD), jnp.bfloat16),
            pltpu.VMEM((NB, ROWS, HD), jnp.float32),
            pltpu.VMEM((NB, ROWS, HD), jnp.float32),
            pltpu.VMEM((NB, ROWS, HD), jnp.float32),
            dma((3, NH)), dma((NB,)), dma((NB,)), dma((NB,)),
            dma((2, 2, NB)), dma((2, 2, NB)), dma((NB,)), dma((NH,)),
            dma((NZ,)), dma((NZ,)), dma((4,)), dma((4,)), dma((4,)), dma((4,)),
            dma((2,)), dma((2,)), dma((8,)), dma((8,)),
        ],
        compiler_params=pltpu.CompilerParams(collective_id=0, has_side_effects=True,
                                             vmem_limit_bytes=48 * 1024 * 1024),
        name="gather_and_attend",
    )(q, k, v, w)


def per_device(queries, keys, values, hidden, control, gate, out_weight):
    channels = queries.shape[-1]
    width = out_weight.shape[1]
    flat = [a.reshape(-1, channels) for a in (queries, keys, values)]
    attention, weight = gather_and_attend(*flat, out_weight)
    projected = jnp.dot(attention, weight.reshape(channels, width), preferred_element_type=jnp.float32)
    result = hidden.reshape(-1, width).astype(jnp.float32) + gate.astype(jnp.float32)[None, :] * projected
    result = result + control.reshape(-1, width).astype(jnp.float32)
    return result.astype(jnp.bfloat16).reshape(hidden.shape)


def solution(mesh):
    tokens = P(("batch", "frame"), "space", None, None, None)
    return jax.shard_map(
        per_device,
        mesh=mesh,
        in_specs=(tokens,) * 5 + (P(), P(("frame", "space"), None)),
        out_specs=tokens,
        check_vma=False,
    )
```

time: 497 us -> 119 us (0.24)
  the two profiles are of different devices: /device:TPU:123 before, /device:TPU:70 now
where the time goes in v1:
time: 119 us
  Pallas kernels  108 us (91%)
  matrix products  6.42 us (5%)
  local copies, waits for them, and re-layouts  3.9 us (3%)
    pallas_call x1, Pallas kernels, gather_and_attend(): pl.pallas_call(kernel, out_shape=(jax.ShapeDtypeStruct(q.shape, q.dtype),...  108 us
    dot_general x1, matrix products, per_device(): jnp.dot(attention, weight.reshape(channels, width), preferred_element_typ...  6.42 us
    unnamed x10, local copies, waits for them, and re-layouts  3.9 us

profile of v1, /device:TPU:70, one launch (start us, length us, event | category | flops | bytes accessed | tf_op | source)
XLA Modules:
  0.0 118.9 jit_solution(8973613523672227694)
XLA Ops:
  0.0 0.7 convert_element_type.20
  0.7 0.0 copy-start
  0.7 1.0 copy-done
  1.7 0.0 copy-start.1
  1.7 1.0 copy-done.1
  2.7 0.0 copy-start.2
  2.7 1.0 copy-done.2
  3.7 0.0 copy-start.3
  3.7 0.9 copy-done.3
  4.6 0.0 copy-start.4
  4.6 107.9 %gather_and_attend.1 = (bf16[128,1536]{1,0:T(8,128)(2,1)S(1)}, bf16[4,16,24,3072]{3,2,1,0:T(8,128)(2,1)}) custom-call(bf16[128,1536]{1,0:T(8,128)(2,1)S(1)} %bitcast.13, bf16[128,1536]{1,0:T(8,128)(2,1)S(1)} %bitcast.14, bf16[128,1536]{1,0:T(8,128)(2,1)S(1)} %bitcast.15, bf16[24,3072]{1,0:T(8,128)(2,1)S(1)} %copy-done.3), custom_call_target="tpu_custom_call" | custom-call | tf_op jit(solution)/shard_map/gather_and_attend/pallas_call | solution.py:341
  112.5 0.0 copy-done.4
  112.5 6.4 %fusion.2 = bf16[128,3072]{1,0:T(8,128)(2,1)} fusion(bf16[128,1536]{1,0:T(8,128)(2,1)S(1)} %get-tuple-element.7, bf16[1536,3072]{1,0:T(8,128)(2,1)} %bitcast.16, bf16[128,3072]{1,0:T(8,128)(2,1)S(1)} %bitcast.17, bf16[128,3072]{1,0:T(8,128)(2,1)} %bitcast.18, f32[3072]{0:T(1024)S(1)} %convert_element_type.20), kind=kOutput, calls=%fused_computation.3 | convolution fusion | flops 1210318848 | bytes 12201984 | tf_op jit(solution)/shard_map/dot_general | solution.py:371
Async XLA Ops:
  0.7 1.0 copy-start
  1.7 1.0 copy-start.1
  2.7 1.0 copy-start.2
  3.7 0.9 copy-start.3
  4.6 107.9 %copy-start.4 = (bf16[2,1,8,8,3072]{4,3,2,1,0:T(8,128)(2,1)S(1)}, bf16[2,1,8,8,3072]{4,3,2,1,0:T(8,128)(2,1)}, u32[]{:S(2)}) copy-start(bf16[2,1,8,8,3072]{4,3,2,1,0:T(8,128)(2,1)} %param.11) | copy-start | bytes 2359300

commit v2 on v1

--- a/solution.py
+++ b/solution.py
@@ -19,13 +19,8 @@
 SCALE = HD ** -0.5 * 1.4426950408889634
 
 
-def window(box):
-    r, c = box // GW, box % GW
-    return range(max(r - 1, 0), min(r + 2, GW)), max(c - 1, 0), min(c + 2, GW)
-
-
 def kernel(q_hbm, k_hbm, v_hbm, w_hbm, attn, wfull,
-           qbuf, kbuf, vbuf, obuf, mbuf, lbuf, acc,
+           qbuf, kbuf, vbuf, vturn, obuf, sbuf, mbuf, abuf, lbuf, acc,
            s_snd, k_rcv, v_rcv, q_rcv, h_snd, h_rcv, o_snd, o_rcv,
            w1s, w1r, w2s, w2r, w3s, w3r, w4s, w4r, w5s, w5r):
     y, f, s = lax.axis_index("batch"), lax.axis_index("frame"), lax.axis_index("space")
@@ -221,60 +216,99 @@
             else:
                 cp.wait_send()
 
+    spans = ((0, 2), (0, 3), (0, 3), (1, 3))
+
+    def around(k):
+        r = k // 2
+        return r, k % 2, range(max(r - 1, 0), min(r + 2, GW))
+
+    def score(j, k):
+        r, pair, rows = around(k)
+        box = r * GW + 2 * pair
+        q = qbuf[box:box + 2].reshape(2 * ROWS, HD)
+        tops = [[], []]
+        for i, g in enumerate(rows):
+            sc = lax.dot_general(kbuf[j, g * GW + pair:g * GW + pair + 3].reshape(3 * ROWS, HD), q,
+                                 (((1,), (1,)), ((), ())), preferred_element_type=jnp.float32)
+            sbuf[k % 2, i * 3 * ROWS:(i + 1) * 3 * ROWS] = sc
+            for side in (0, 1):
+                k0, k1 = spans[2 * pair + side]
+                tops[side].append(jnp.max(sc[k0 * ROWS:k1 * ROWS, side * ROWS:side * ROWS + ROWS],
+                                          axis=0, keepdims=True))
+        for side in (0, 1):
+            m_old = mbuf[box + side]
+            m_new = functools.reduce(jnp.maximum, tops[side], m_old)
+            mbuf[box + side] = m_new
+            abuf[box + side] = jnp.exp2((m_old - m_new) * SCALE)
+
+    def blend(k):
+        r, pair, rows = around(k)
+        for side in (0, 1):
+            box = r * GW + 2 * pair + side
+            k0, k1 = spans[2 * pair + side]
+            shift = mbuf[box] * SCALE
+            total = lbuf[box] * abuf[box]
+            out = acc[box] * abuf[box]
+            for i, g in enumerate(rows):
+                sc = sbuf[k % 2, (3 * i + k0) * ROWS:(3 * i + k1) * ROWS, side * ROWS:side * ROWS + ROWS]
+                p = jnp.exp2(sc * SCALE - shift)
+                total = total + jnp.sum(p, axis=0, keepdims=True)
+                c = (g * GW + pair + k0) * ROWS
+                out = out + jnp.dot(vturn[:, c:c + (k1 - k0) * ROWS], p.astype(jnp.bfloat16),
+                                    preferred_element_type=jnp.float32)
+            lbuf[box] = total
+            acc[box] = out
+
+    def finish(r):
+        for box in range(r * GW, r * GW + GW):
+            obuf[box] = (acc[box] / lbuf[box]).T.astype(jnp.bfloat16)
+        for box in range(r * GW - GW, r * GW):
+            if box >= 0:
+                send_o(box, True)
+
     def one_frame(j, carry):
         @pl.when(j == 1)
         def _():
             relay_weight()
 
-        for box in range(NB):
-            rows, c0, c1 = window(box)
-            if box % GW == 0:
-                fresh = (0, 1) if box == 0 else ((box // GW + 1,) if box // GW + 1 < GW else ())
-
-                @pl.when(j > 0)
-                def _():
-                    for r in fresh:
-                        for b in range(r * GW, r * GW + GW):
-                            await_copy(kbuf.at[j, b], h_rcv.at[0, j - 1, b])
-                            await_copy(vbuf.at[j, b], h_rcv.at[1, j - 1, b])
+        for r in range(GW):
+            fresh = range(0, 2) if r == 0 else range(r + 1, min(r + 2, GW))
+
+            @pl.when(j > 0)
+            def _():
+                for b in (g * GW + c for g in fresh for c in range(GW)):
+                    await_copy(kbuf.at[j, b], h_rcv.at[0, j - 1, b])
+                    await_copy(vbuf.at[j, b], h_rcv.at[1, j - 1, b])
 
             @pl.when(j == 0)
             def _():
-                await_copy(qbuf.at[box], q_rcv.at[box])
-
-            n = (c1 - c0) * ROWS
-            q = qbuf[box]
-            scores = [lax.dot_general(q, kbuf[j, r * GW + c0:r * GW + c1].reshape(n, HD),
-                                      (((1,), (1,)), ((), ())), preferred_element_type=jnp.float32)
-                      for r in rows]
-            top = functools.reduce(jnp.maximum, scores)
-            m_old = mbuf[box]
-            m_new = jnp.maximum(m_old, jnp.max(top, axis=1, keepdims=True))
-            alpha = jnp.exp2((m_old - m_new) * SCALE)
-            shift = m_new[:, :1] * SCALE
-            total = lbuf[box] * alpha
-            out = acc[box] * alpha
-            for r, sc in zip(rows, scores):
-                p = jnp.exp2(sc * SCALE - shift)
-                total = total + jnp.sum(p, axis=1, keepdims=True)
-                out = out + jnp.dot(p.astype(jnp.bfloat16),
-                                    vbuf[j, r * GW + c0:r * GW + c1].reshape(n, HD),
-                                    preferred_element_type=jnp.float32)
-            mbuf[box] = m_new
-            lbuf[box] = total
-            acc[box] = out
-
-            @pl.when(j == frames - 1)
-            def _():
-                obuf[box] = (out / total).astype(jnp.bfloat16)
-                if box:
-                    send_o(box - 1, True)
+                for box in range(r * GW, r * GW + GW):
+                    await_copy(qbuf.at[box], q_rcv.at[box])
+
+            for b in (g * GW + c for g in fresh for c in range(GW)):
+                vturn[:, b * ROWS:b * ROWS + ROWS] = vbuf[j, b].T
+            score(j, 2 * r)
+            if r:
+                blend(2 * r - 1)
+
+                @pl.when(j == frames - 1)
+                def _():
+                    finish(r - 1)
+            score(j, 2 * r + 1)
+            blend(2 * r)
+
+        blend(2 * GW - 1)
+
+        @pl.when(j == frames - 1)
+        def _():
+            finish(GW - 1)
         return carry
 
     @pl.when(owner)
     def _():
         lax.fori_loop(0, frames, one_frame, 0)
-        send_o(NB - 1, True)
+        for box in range(NB - GW, NB):
+            send_o(box, True)
 
     @pl.when(jnp.logical_not(owner))
     def _():
@@ -348,17 +382,20 @@
             pltpu.VMEM((NB, ROWS, HD), jnp.bfloat16),
             pltpu.VMEM((3, NB, ROWS, HD), jnp.bfloat16),
             pltpu.VMEM((3, NB, ROWS, HD), jnp.bfloat16),
+            pltpu.VMEM((HD, NB * ROWS), jnp.bfloat16),
             pltpu.VMEM((NB, ROWS, HD), jnp.bfloat16),
-            pltpu.VMEM((NB, ROWS, HD), jnp.float32),
-            pltpu.VMEM((NB, ROWS, HD), jnp.float32),
-            pltpu.VMEM((NB, ROWS, HD), jnp.float32),
+            pltpu.VMEM((2, 9 * ROWS, 2 * ROWS), jnp.float32),
+            pltpu.VMEM((NB, 1, ROWS), jnp.float32),
+            pltpu.VMEM((NB, 1, ROWS), jnp.float32),
+            pltpu.VMEM((NB, 1, ROWS), jnp.float32),
+            pltpu.VMEM((NB, HD, ROWS), jnp.float32),
             dma((3, NH)), dma((NB,)), dma((NB,)), dma((NB,)),
             dma((2, 2, NB)), dma((2, 2, NB)), dma((NB,)), dma((NH,)),
             dma((NZ,)), dma((NZ,)), dma((4,)), dma((4,)), dma((4,)), dma((4,)),
             dma((2,)), dma((2,)), dma((8,)), dma((8,)),
         ],
         compiler_params=pltpu.CompilerParams(collective_id=0, has_side_effects=True,
-                                             vmem_limit_bytes=48 * 1024 * 1024),
+                                             vmem_limit_bytes=62 * 1024 * 1024),
         name="gather_and_attend",
     )(q, k, v, w)
 

time: 119 us -> 108 us (0.908)
  the two profiles are of different devices: /device:TPU:70 before, /device:TPU:6 now
where the time goes in v2:
time: 108 us
  Pallas kernels  101 us (94%)
  matrix products  6.54 us (6%)
    pallas_call x1, Pallas kernels, gather_and_attend(): pl.pallas_call(kernel, out_shape=(jax.ShapeDtypeStruct(q.shape, q.dtype),...  101 us
    dot_general x1, matrix products, per_device(): jnp.dot(attention, weight.reshape(channels, width), preferred_element_typ...  6.54 us

profile of v2, /device:TPU:6, one launch (start us, length us, event | category | flops | bytes accessed | tf_op | source)
XLA Modules:
  0.0 107.9 jit_solution(18437050624042339054)
XLA Ops:
  0.0 0.0 copy-start
  0.0 0.8 convert_element_type.20
  0.8 100.6 %gather_and_attend.1 = (bf16[128,1536]{1,0:T(8,128)(2,1)}, bf16[4,16,24,3072]{3,2,1,0:T(8,128)(2,1)}) custom-call(bf16[128,1536]{1,0:T(8,128)(2,1)} %bitcast.16, bf16[128,1536]{1,0:T(8,128)(2,1)} %bitcast.17, bf16[128,1536]{1,0:T(8,128)(2,1)} %bitcast.18, bf16[24,3072]{1,0:T(8,128)(2,1)} %w_hbm.1), custom_call_target="tpu_custom_call" | custom-call | tf_op jit(solution)/shard_map/gather_and_attend/pallas_call | solution.py:375
  101.4 0.0 copy-done
  101.4 6.5 %fusion.2 = bf16[128,3072]{1,0:T(8,128)(2,1)} fusion(bf16[128,1536]{1,0:T(8,128)(2,1)} %get-tuple-element.7, bf16[1536,3072]{1,0:T(8,128)(2,1)} %bitcast.13, bf16[128,3072]{1,0:T(8,128)(2,1)S(1)} %bitcast.14, bf16[128,3072]{1,0:T(8,128)(2,1)} %bitcast.15, f32[3072]{0:T(1024)S(1)} %convert_element_type.20), kind=kOutput, calls=%fused_computation.3 | convolution fusion | flops 1210318848 | bytes 12201984 | tf_op jit(solution)/shard_map/dot_general | solution.py:408
Async XLA Ops:
  0.0 101.4 %copy-start = (bf16[2,1,8,8,3072]{4,3,2,1,0:T(8,128)(2,1)S(1)}, bf16[2,1,8,8,3072]{4,3,2,1,0:T(8,128)(2,1)}, u32[]{:S(2)}) copy-start(bf16[2,1,8,8,3072]{4,3,2,1,0:T(8,128)(2,1)} %param.11) | copy-start | bytes 2359300

commit v3 on v2

--- a/solution.py
+++ b/solution.py
@@ -27,8 +27,8 @@
     lo, z = s // NZ, s % NZ
     hi, core = f // 2, f % 2
     quarter = wfull.shape[-1] // NY
-    owner = s % 4 != 3
-    my_head = (s // 4) * 3 + s % 4
+    owner = jnp.where(s < NZ, s % 4 != 3, s % 4 != 1)
+    my_head = (s // 4) * 3 + s % 4 - jnp.where((s >= NZ) & (s % 4 > 1), 1, 0)
     partner = f + 1 - 2 * core
     cross = f - 1 + 2 * core
     has_cross = (f == 1) | (f == 2)
@@ -78,11 +78,11 @@
     pltpu.make_async_copy(w_hbm.at[:, wcols(y)], wfull.at[f, s, :, wcols(y)], w1r.at[z]).start()
     lax.fori_loop(1, NZ, start_w1, 0)
 
-    first = (s // 4) * 3 + jnp.minimum(s % 4, 2)
+    first = jnp.minimum(my_head, NH - 1)
 
     def head_of(i):
         h = (first + i) % NH
-        return h, (h // 3) * 4 + h % 3
+        return h, (h // 3) * 4 + h % 3 + jnp.where((h >= NH // 2) & (h % 3 > 0), 1, 0)
 
     def piece(ref, h):
         return ref.at[:, pl.ds(pl.multiple_of(h * HD, HD), HD)]
@@ -109,21 +109,72 @@
     send_heads((0, 1))
     send_heads((2,))
 
+    places = (x, xl, xr, (x + 2) % 4)
+    layers = (y, yl, yr, (y + 2) % NY)
+    halves = ((0, NZ // 2), (NZ // 2, NZ // 2))
+
+    def block(n, m=0, side=core, part=(0, NZ)):
+        pos = places[n]
+        return wfull.at[(pos // 2) * 2 + side, pl.ds((pos % 2) * NZ + part[0], part[1]), :, wcols(layers[m])]
+
+    def push(ref, snd, rcv, dev):
+        return remote(ref, ref, snd, rcv, dev)
+
+    x_own = (push(block(0), w2s.at[0], w2r.at[0], at_x(xr)), push(block(0), w2s.at[1], w2r.at[1], at_x(xl)))
+    x_rel = (push(block(1, part=halves[0]), w2s.at[2], w2r.at[2], at_x(xr)),
+             push(block(2, part=halves[1]), w2s.at[3], w2r.at[3], at_x(xl)))
+
+    def y_own(d, n):
+        return push(block(n), w3s.at[4 * d + n], w3r.at[4 * d + n], ((yr, yl)[d], f, s))
+
+    def y_rel(n):
+        return push(block(n, 1), w4s.at[n], w4r.at[n], (yr, f, s)) if n < 2 else \
+            push(block(n, 2), w4s.at[n], w4r.at[n], (yl, f, s))
+
+    def to_partner(m, n):
+        return push(block(n, m), w5s.at[4 * m + n], w5r.at[4 * m + n], (y, partner, s))
+
+    def spread(n):
+        y_own(0, n).start()
+        y_own(1, n).start()
+        to_partner(0, n).start()
+
+    def weight_z():
+        lax.fori_loop(0, NZ, await_w1, 0)
+        x_own[0].start()
+        x_own[1].start()
+        spread(0)
+
+    def weight_x():
+        await_copy(block(1), w2r.at[0])
+        x_rel[0].start()
+        spread(1)
+        await_copy(block(2), w2r.at[1])
+        x_rel[1].start()
+        spread(2)
+
+    def weight_x2():
+        await_copy(block(3, part=halves[0]), w2r.at[2])
+        await_copy(block(3, part=halves[1]), w2r.at[3])
+        spread(3)
+
+    def weight_y(n):
+        await_copy(block(n, 1), w3r.at[n])
+        if n < 2:
+            y_rel(n).start()
+        to_partner(1, n).start()
+        await_copy(block(n, 2), w3r.at[4 + n])
+        if n >= 2:
+            y_rel(n).start()
+        to_partner(2, n).start()
+
+    def weight_y2(n):
+        await_copy(block(n, 3), w4r.at[n])
+        to_partner(3, n).start()
+
     def await_w1(i, carry):
         await_copy(wfull.at[f, lo * NZ + i, :, wcols(y)], w1r.at[i])
         return carry
-
-    lax.fori_loop(0, NZ, await_w1, 0)
-
-    def xblock(pos, start=0, count=NZ):
-        return wfull.at[(pos // 2) * 2 + core, pl.ds((pos % 2) * NZ + start, count), :, wcols(y)]
-
-    own_r = remote(xblock(x), xblock(x), w2s.at[0], w2r.at[0], at_x(xr))
-    own_l = remote(xblock(x), xblock(x), w2s.at[1], w2r.at[1], at_x(xl))
-    rel_r = remote(xblock(xl, 0, 4), xblock(xl, 0, 4), w2s.at[2], w2r.at[2], at_x(xr))
-    rel_l = remote(xblock(xr, 4, 4), xblock(xr, 4, 4), w2s.at[3], w2r.at[3], at_x(xl))
-    own_r.start()
-    own_l.start()
 
     def forward(i):
         box = (s + NB - i) % NB
@@ -147,58 +198,24 @@
             near.start()
         return carry
 
+    weight_steps = (weight_z, weight_x, weight_x2) + tuple(functools.partial(weight_y, n) for n in range(4))
+
     @pl.when(owner)
     def _():
         mbuf[...] = jnp.full_like(mbuf, -1e30)
         lbuf[...] = jnp.zeros_like(lbuf)
         acc[...] = jnp.zeros_like(acc)
-        lax.fori_loop(0, 8, forward_step, 0)
-
-    await_copy(xblock(xl), w2r.at[0])
-    await_copy(xblock(xr), w2r.at[1])
-    rel_r.start()
-    rel_l.start()
-
-    @pl.when(owner)
+        marks = (0, 2, 4, 6, 8, 11, 14, NB)
+        for step, i0, i1 in zip(weight_steps, marks, marks[1:]):
+            step()
+            lax.fori_loop(i0, i1, forward_step, 0)
+
+    @pl.when(jnp.logical_not(owner))
     def _():
-        lax.fori_loop(8, NB, forward_step, 0)
-
-    x2 = (x + 2) % 4
-    await_copy(xblock(x2, 0, 4), w2r.at[2])
-    await_copy(xblock(x2, 4, 4), w2r.at[3])
-
-    def wblock(yy, n, side):
-        return wfull.at[side + 2 * n, :, :, wcols(yy)]
-
-    y2 = (y + 2) % NY
-
-    def to_partner(n, m):
-        yy = (y, yl, yr, y2)[n]
-        return remote(wblock(yy, m, core), wblock(yy, m, core), w5s.at[2 * n + m], w5r.at[2 * n + m],
-                      (y, partner, s))
-
-    def y_own(d, m):
-        return remote(wblock(y, m, core), wblock(y, m, core), w3s.at[2 * d + m], w3r.at[2 * d + m],
-                      ((yr, yl)[d], f, s))
-
-    y_rel = (remote(wblock(yl, 0, core), wblock(yl, 0, core), w4s.at[0], w4r.at[0], (yr, f, s)),
-             remote(wblock(yr, 1, core), wblock(yr, 1, core), w4s.at[1], w4r.at[1], (yl, f, s)))
-    for d, m in ((0, 0), (1, 1), (0, 1), (1, 0)):
-        y_own(d, m).start()
-    for m in (0, 1):
-        to_partner(0, m).start()
-
-    def relay_weight():
-        await_copy(wblock(yl, 0, core), w3r.at[0])
-        y_rel[0].start()
-        await_copy(wblock(yr, 1, core), w3r.at[3])
-        y_rel[1].start()
-        to_partner(1, 0).start()
-        to_partner(2, 1).start()
-        await_copy(wblock(yl, 1, core), w3r.at[1])
-        to_partner(1, 1).start()
-        await_copy(wblock(yr, 0, core), w3r.at[2])
-        to_partner(2, 0).start()
+        for step in weight_steps:
+            step()
+        for n in range(4):
+            weight_y2(n)
 
     frames = jnp.where(has_cross, 3, 2)
 
@@ -241,7 +258,7 @@
             mbuf[box + side] = m_new
             abuf[box + side] = jnp.exp2((m_old - m_new) * SCALE)
 
-    def blend(k):
+    def blend(j, k):
         r, pair, rows = around(k)
         for side in (0, 1):
             box = r * GW + 2 * pair + side
@@ -254,7 +271,7 @@
                 p = jnp.exp2(sc * SCALE - shift)
                 total = total + jnp.sum(p, axis=0, keepdims=True)
                 c = (g * GW + pair + k0) * ROWS
-                out = out + jnp.dot(vturn[:, c:c + (k1 - k0) * ROWS], p.astype(jnp.bfloat16),
+                out = out + jnp.dot(vturn[j, :, c:c + (k1 - k0) * ROWS], p.astype(jnp.bfloat16),
                                     preferred_element_type=jnp.float32)
             lbuf[box] = total
             acc[box] = out
@@ -262,71 +279,60 @@
     def finish(r):
         for box in range(r * GW, r * GW + GW):
             obuf[box] = (acc[box] / lbuf[box]).T.astype(jnp.bfloat16)
-        for box in range(r * GW - GW, r * GW):
-            if box >= 0:
-                send_o(box, True)
-
-    def one_frame(j, carry):
-        @pl.when(j == 1)
+
+    def send_row(r):
+        for box in range(r * GW, r * GW + GW):
+            send_o(box, True)
+
+    def attend_row(r):
+        fresh = [g * GW + c for g in (range(0, 2) if r == 0 else range(r + 1, min(r + 2, GW))) for c in range(GW)]
+
+        def await_halo(j):
+            for b in fresh:
+                await_copy(kbuf.at[j, b], h_rcv.at[0, j - 1, b])
+                await_copy(vbuf.at[j, b], h_rcv.at[1, j - 1, b])
+
+        await_halo(1)
+
+        @pl.when(has_cross)
         def _():
-            relay_weight()
-
-        for r in range(GW):
-            fresh = range(0, 2) if r == 0 else range(r + 1, min(r + 2, GW))
-
-            @pl.when(j > 0)
-            def _():
-                for b in (g * GW + c for g in fresh for c in range(GW)):
-                    await_copy(kbuf.at[j, b], h_rcv.at[0, j - 1, b])
-                    await_copy(vbuf.at[j, b], h_rcv.at[1, j - 1, b])
-
-            @pl.when(j == 0)
-            def _():
-                for box in range(r * GW, r * GW + GW):
-                    await_copy(qbuf.at[box], q_rcv.at[box])
-
-            for b in (g * GW + c for g in fresh for c in range(GW)):
-                vturn[:, b * ROWS:b * ROWS + ROWS] = vbuf[j, b].T
-            score(j, 2 * r)
-            if r:
-                blend(2 * r - 1)
-
-                @pl.when(j == frames - 1)
-                def _():
-                    finish(r - 1)
+            await_halo(2)
+
+        for box in range(r * GW, r * GW + GW):
+            await_copy(qbuf.at[box], q_rcv.at[box])
+        score(0, 2 * r)
+        if r:
+            send_row(r - 1)
+
+        def one_frame(j, carry):
+            for b in fresh:
+                vturn[j, :, b * ROWS:b * ROWS + ROWS] = vbuf[j, b].T
             score(j, 2 * r + 1)
-            blend(2 * r)
-
-        blend(2 * GW - 1)
-
-        @pl.when(j == frames - 1)
-        def _():
-            finish(GW - 1)
-        return carry
+            blend(j, 2 * r)
+            score(jnp.minimum(j + 1, frames - 1), 2 * r)
+            blend(j, 2 * r + 1)
+            return carry
+
+        lax.fori_loop(0, frames, one_frame, 0)
+        finish(r)
 
     @pl.when(owner)
     def _():
-        lax.fori_loop(0, frames, one_frame, 0)
-        for box in range(NB - GW, NB):
-            send_o(box, True)
-
-    @pl.when(jnp.logical_not(owner))
-    def _():
-        relay_weight()
-
-    await_copy(wblock(y2, 0, core), w4r.at[0])
-    to_partner(3, 0).start()
-    await_copy(wblock(y2, 1, core), w4r.at[1])
-    to_partner(3, 1).start()
+        for r in range(GW):
+            attend_row(r)
+            if r >= 2:
+                weight_y2(2 * r - 4)
+                weight_y2(2 * r - 3)
+        send_row(GW - 1)
 
     def await_o(h, carry):
         await_copy(piece(attn, h), o_rcv.at[h])
         return carry
 
     lax.fori_loop(0, NH, await_o, 0)
-    for n in range(4):
-        for m in (0, 1):
-            await_copy(wblock((y, yl, yr, y2)[n], m, 1 - core), w5r.at[2 * n + m])
+    for m in range(4):
+        for n in range(4):
+            await_copy(block(n, m, 1 - core), w5r.at[4 * m + n])
 
     def drain_heads(i, carry):
         h, to = head_of(i)
@@ -344,14 +350,14 @@
         return carry
 
     lax.fori_loop(1, NZ, drain_w1, 0)
-    for cp in (own_r, own_l, rel_r, rel_l) + y_rel:
+    for cp in x_own + x_rel:
         cp.wait_send()
-    for d in (0, 1):
-        for m in (0, 1):
-            y_own(d, m).wait_send()
     for n in range(4):
-        for m in (0, 1):
-            to_partner(n, m).wait_send()
+        y_own(0, n).wait_send()
+        y_own(1, n).wait_send()
+        y_rel(n).wait_send()
+        for m in range(4):
+            to_partner(m, n).wait_send()
 
     @pl.when(owner)
     def _():
@@ -382,7 +388,7 @@
             pltpu.VMEM((NB, ROWS, HD), jnp.bfloat16),
             pltpu.VMEM((3, NB, ROWS, HD), jnp.bfloat16),
             pltpu.VMEM((3, NB, ROWS, HD), jnp.bfloat16),
-            pltpu.VMEM((HD, NB * ROWS), jnp.bfloat16),
+            pltpu.VMEM((3, HD, NB * ROWS), jnp.bfloat16),
             pltpu.VMEM((NB, ROWS, HD), jnp.bfloat16),
             pltpu.VMEM((2, 9 * ROWS, 2 * ROWS), jnp.float32),
             pltpu.VMEM((NB, 1, ROWS), jnp.float32),
@@ -391,8 +397,8 @@
             pltpu.VMEM((NB, HD, ROWS), jnp.float32),
             dma((3, NH)), dma((NB,)), dma((NB,)), dma((NB,)),
             dma((2, 2, NB)), dma((2, 2, NB)), dma((NB,)), dma((NH,)),
-            dma((NZ,)), dma((NZ,)), dma((4,)), dma((4,)), dma((4,)), dma((4,)),
-            dma((2,)), dma((2,)), dma((8,)), dma((8,)),
+            dma((NZ,)), dma((NZ,)), dma((4,)), dma((4,)), dma((8,)), dma((8,)),
+            dma((4,)), dma((4,)), dma((16,)), dma((16,)),
         ],
         compiler_params=pltpu.CompilerParams(collective_id=0, has_side_effects=True,
                                              vmem_limit_bytes=62 * 1024 * 1024),

time: 108 us -> 89.8 us (0.83)
  the two profiles are of different devices: /device:TPU:6 before, /device:TPU:3 now
where the time goes in v3:
time: 89.8 us; the launch traced here: 89.7 us
  Pallas kernels  82.4 us (92%)
  matrix products  6.54 us (7%)
    pallas_call x1, Pallas kernels, gather_and_attend(): pl.pallas_call(kernel, out_shape=(jax.ShapeDtypeStruct(q.shape, q.dtype),...  82.4 us
    dot_general x1, matrix products, per_device(): jnp.dot(attention, weight.reshape(channels, width), preferred_element_typ...  6.54 us

profile of v3, /device:TPU:3, one launch (start us, length us, event | category | flops | bytes accessed | tf_op | source)
XLA Modules:
  0.0 89.7 jit_solution(14158949484614686729)
XLA Ops:
  0.0 0.0 copy-start
  0.0 0.8 convert_element_type.20
  0.8 82.4 %gather_and_attend.1 = (bf16[128,1536]{1,0:T(8,128)(2,1)}, bf16[4,16,24,3072]{3,2,1,0:T(8,128)(2,1)}) custom-call(bf16[128,1536]{1,0:T(8,128)(2,1)} %bitcast.16, bf16[128,1536]{1,0:T(8,128)(2,1)} %bitcast.17, bf16[128,1536]{1,0:T(8,128)(2,1)} %bitcast.18, bf16[24,3072]{1,0:T(8,128)(2,1)} %w_hbm.1), custom_call_target="tpu_custom_call" | custom-call | tf_op jit(solution)/shard_map/gather_and_attend/pallas_call | solution.py:381
  83.1 0.0 copy-done
  83.2 6.5 %fusion.2 = bf16[128,3072]{1,0:T(8,128)(2,1)} fusion(bf16[128,1536]{1,0:T(8,128)(2,1)} %get-tuple-element.7, bf16[1536,3072]{1,0:T(8,128)(2,1)} %bitcast.13, bf16[128,3072]{1,0:T(8,128)(2,1)S(1)} %bitcast.14, bf16[128,3072]{1,0:T(8,128)(2,1)} %bitcast.15, f32[3072]{0:T(1024)S(1)} %convert_element_type.20), kind=kOutput, calls=%fused_computation.3 | convolution fusion | flops 1210318848 | bytes 12201984 | tf_op jit(solution)/shard_map/dot_general | solution.py:414
Async XLA Ops:
  0.0 83.2 %copy-start = (bf16[2,1,8,8,3072]{4,3,2,1,0:T(8,128)(2,1)S(1)}, bf16[2,1,8,8,3072]{4,3,2,1,0:T(8,128)(2,1)}, u32[]{:S(2)}) copy-start(bf16[2,1,8,8,3072]{4,3,2,1,0:T(8,128)(2,1)} %param.11) | copy-start | bytes 2359300

commit v4 on v3

--- a/solution.py
+++ b/solution.py
@@ -19,7 +19,7 @@
 SCALE = HD ** -0.5 * 1.4426950408889634
 
 
-def kernel(q_hbm, k_hbm, v_hbm, w_hbm, attn, wfull,
+def kernel(q_hbm, k_hbm, v_hbm, w_ref, attn, wfull,
            qbuf, kbuf, vbuf, vturn, obuf, sbuf, mbuf, abuf, lbuf, acc,
            s_snd, k_rcv, v_rcv, q_rcv, h_snd, h_rcv, o_snd, o_rcv,
            w1s, w1r, w2s, w2r, w3s, w3r, w4s, w4r, w5s, w5r):
@@ -68,33 +68,34 @@
 
     def w1(i):
         zz = (z + i) % NZ
-        return remote(w_hbm.at[:, wcols(y)], wfull.at[f, s, :, wcols(y)], w1s.at[zz], w1r.at[z],
+        return remote(w_ref.at[:, wcols(y)], wfull.at[f, s, :, wcols(y)], w1s.at[zz], w1r.at[z],
                       (y, f, lo * NZ + zz))
 
     def start_w1(i, carry):
         w1(i).start()
         return carry
 
-    pltpu.make_async_copy(w_hbm.at[:, wcols(y)], wfull.at[f, s, :, wcols(y)], w1r.at[z]).start()
+    pltpu.make_async_copy(w_ref.at[:, wcols(y)], wfull.at[f, s, :, wcols(y)], w1r.at[z]).start()
     lax.fori_loop(1, NZ, start_w1, 0)
 
     first = jnp.minimum(my_head, NH - 1)
 
-    def head_of(i):
-        h = (first + i) % NH
-        return h, (h // 3) * 4 + h % 3 + jnp.where((h >= NH // 2) & (h % 3 > 0), 1, 0)
+    half = NH // 2
+
+    def head_of(wave, i):
+        top = lo if wave == 0 else 1 - lo
+        h = top * half + (first + i) % half
+        return h, (h // 3) * 4 + h % 3 + jnp.where((h >= half) & (h % 3 > 0), 1, 0)
 
     def piece(ref, h):
         return ref.at[:, pl.ds(pl.multiple_of(h * HD, HD), HD)]
 
     streams = ((0, k_hbm, kbuf.at[0], k_rcv), (1, v_hbm, vbuf.at[0], v_rcv), (2, q_hbm, qbuf, q_rcv))
 
-    def send_heads(which):
+    def send_heads(wave):
         def step(i, carry):
-            h, to = head_of(i)
-            for n in which:
-                row, src, dst, rcv = streams[n]
-
+            h, to = head_of(wave, i)
+            for row, src, dst, rcv in streams:
                 @pl.when(to == s)
                 def _():
                     pltpu.make_async_copy(piece(src, h), dst.at[s], rcv.at[s]).start()
@@ -104,10 +105,9 @@
                     remote(piece(src, h), dst.at[s], s_snd.at[row, h], rcv.at[s], (y, f, to)).start()
             return carry
 
-        lax.fori_loop(0, NH, step, 0)
-
-    send_heads((0, 1))
-    send_heads((2,))
+        lax.fori_loop(0, half, step, 0)
+
+    send_heads(0)
 
     places = (x, xl, xr, (x + 2) % 4)
     layers = (y, yl, yr, (y + 2) % NY)
@@ -177,7 +177,7 @@
         return carry
 
     def forward(i):
-        box = (s + NB - i) % NB
+        box = ((lo + i // NZ) % 2) * NZ + (z + NB - i) % NZ
         out = []
         for n, (buf, rcv) in enumerate(((kbuf, k_rcv), (vbuf, v_rcv))):
             out.append((buf, rcv, box,
@@ -198,17 +198,20 @@
             near.start()
         return carry
 
-    weight_steps = (weight_z, weight_x, weight_x2) + tuple(functools.partial(weight_y, n) for n in range(4))
+    weight_z()
+    weight_x()
+    send_heads(1)
+    weight_steps = (weight_x2,) + tuple(functools.partial(weight_y, n) for n in range(4))
 
     @pl.when(owner)
     def _():
         mbuf[...] = jnp.full_like(mbuf, -1e30)
         lbuf[...] = jnp.zeros_like(lbuf)
         acc[...] = jnp.zeros_like(acc)
-        marks = (0, 2, 4, 6, 8, 11, 14, NB)
-        for step, i0, i1 in zip(weight_steps, marks, marks[1:]):
-            step()
-            lax.fori_loop(i0, i1, forward_step, 0)
+        weight_steps[0]()
+        lax.fori_loop(0, 4, forward_step, 0)
+        weight_steps[1]()
+        lax.fori_loop(4, NZ, forward_step, 0)
 
     @pl.when(jnp.logical_not(owner))
     def _():
@@ -219,15 +222,15 @@
 
     frames = jnp.where(has_cross, 3, 2)
 
-    def send_o(box, start):
+    def send_o(slot, box, start):
         @pl.when(s == box)
         def _():
             if start:
-                pltpu.make_async_copy(obuf.at[box], piece(attn, my_head), o_rcv.at[my_head]).start()
+                pltpu.make_async_copy(obuf.at[slot], piece(attn, my_head), o_rcv.at[my_head]).start()
 
         @pl.when(s != box)
         def _():
-            cp = remote(obuf.at[box], piece(attn, my_head), o_snd.at[box], o_rcv.at[my_head], (y, f, box))
+            cp = remote(obuf.at[slot], piece(attn, my_head), o_snd.at[slot], o_rcv.at[my_head], (y, f, box))
             if start:
                 cp.start()
             else:
@@ -235,19 +238,17 @@
 
     spans = ((0, 2), (0, 3), (0, 3), (1, 3))
 
-    def around(k):
-        r = k // 2
-        return r, k % 2, range(max(r - 1, 0), min(r + 2, GW))
-
-    def score(j, k):
-        r, pair, rows = around(k)
+    def at_row(g):
+        return jnp.where(lo == 0, g, GW - 1 - g) * GW
+
+    def score(j, r, pair, rows, slot):
         box = r * GW + 2 * pair
-        q = qbuf[box:box + 2].reshape(2 * ROWS, HD)
+        q = qbuf[pl.ds(at_row(r) + 2 * pair, 2)].reshape(2 * ROWS, HD)
         tops = [[], []]
         for i, g in enumerate(rows):
-            sc = lax.dot_general(kbuf[j, g * GW + pair:g * GW + pair + 3].reshape(3 * ROWS, HD), q,
+            sc = lax.dot_general(kbuf[j, pl.ds(at_row(g) + pair, 3)].reshape(3 * ROWS, HD), q,
                                  (((1,), (1,)), ((), ())), preferred_element_type=jnp.float32)
-            sbuf[k % 2, i * 3 * ROWS:(i + 1) * 3 * ROWS] = sc
+            sbuf[slot, i * 3 * ROWS:(i + 1) * 3 * ROWS] = sc
             for side in (0, 1):
                 k0, k1 = spans[2 * pair + side]
                 tops[side].append(jnp.max(sc[k0 * ROWS:k1 * ROWS, side * ROWS:side * ROWS + ROWS],
@@ -258,8 +259,7 @@
             mbuf[box + side] = m_new
             abuf[box + side] = jnp.exp2((m_old - m_new) * SCALE)
 
-    def blend(j, k):
-        r, pair, rows = around(k)
+    def blend(j, r, pair, rows, slot):
         for side in (0, 1):
             box = r * GW + 2 * pair + side
             k0, k1 = spans[2 * pair + side]
@@ -267,7 +267,7 @@
             total = lbuf[box] * abuf[box]
             out = acc[box] * abuf[box]
             for i, g in enumerate(rows):
-                sc = sbuf[k % 2, (3 * i + k0) * ROWS:(3 * i + k1) * ROWS, side * ROWS:side * ROWS + ROWS]
+                sc = sbuf[slot, (3 * i + k0) * ROWS:(3 * i + k1) * ROWS, side * ROWS:side * ROWS + ROWS]
                 p = jnp.exp2(sc * SCALE - shift)
                 total = total + jnp.sum(p, axis=0, keepdims=True)
                 c = (g * GW + pair + k0) * ROWS
@@ -281,49 +281,66 @@
             obuf[box] = (acc[box] / lbuf[box]).T.astype(jnp.bfloat16)
 
     def send_row(r):
-        for box in range(r * GW, r * GW + GW):
-            send_o(box, True)
-
-    def attend_row(r):
-        fresh = [g * GW + c for g in (range(0, 2) if r == 0 else range(r + 1, min(r + 2, GW))) for c in range(GW)]
-
-        def await_halo(j):
-            for b in fresh:
-                await_copy(kbuf.at[j, b], h_rcv.at[0, j - 1, b])
-                await_copy(vbuf.at[j, b], h_rcv.at[1, j - 1, b])
-
-        await_halo(1)
+        for c in range(GW):
+            send_o(r * GW + c, at_row(r) + c, True)
+
+    def await_rows(rows):
+        def at_j(j, g, c):
+            b = at_row(g) + c
+            await_copy(kbuf.at[j, b], h_rcv.at[0, j - 1, b])
+            await_copy(vbuf.at[j, b], h_rcv.at[1, j - 1, b])
+
+        for g in rows:
+            for c in range(GW):
+                at_j(1, g, c)
+                await_copy(qbuf.at[at_row(g) + c], q_rcv.at[at_row(g) + c])
 
         @pl.when(has_cross)
         def _():
-            await_halo(2)
-
-        for box in range(r * GW, r * GW + GW):
-            await_copy(qbuf.at[box], q_rcv.at[box])
-        score(0, 2 * r)
-        if r:
-            send_row(r - 1)
+            for g in rows:
+                for c in range(GW):
+                    at_j(2, g, c)
+
+    def attend(r, rows, fresh=()):
+        score(0, r, 0, rows, 0)
 
         def one_frame(j, carry):
-            for b in fresh:
-                vturn[j, :, b * ROWS:b * ROWS + ROWS] = vbuf[j, b].T
-            score(j, 2 * r + 1)
-            blend(j, 2 * r)
-            score(jnp.minimum(j + 1, frames - 1), 2 * r)
-            blend(j, 2 * r + 1)
+            for b in (g * GW + c for g in fresh for c in range(GW)):
+                vturn[j, :, b * ROWS:b * ROWS + ROWS] = vbuf[j, at_row(b // GW) + b % GW].T
+            score(j, r, 1, rows, 1)
+            blend(j, r, 0, rows, 0)
+            score(jnp.minimum(j + 1, frames - 1), r, 0, rows, 0)
+            blend(j, r, 1, rows, 1)
             return carry
 
         lax.fori_loop(0, frames, one_frame, 0)
-        finish(r)
 
     @pl.when(owner)
     def _():
-        for r in range(GW):
-            attend_row(r)
-            if r >= 2:
-                weight_y2(2 * r - 4)
-                weight_y2(2 * r - 3)
-        send_row(GW - 1)
+        await_rows((0, 1))
+        attend(0, (0, 1), (0, 1))
+        finish(0)
+        weight_steps[2]()
+        lax.fori_loop(NZ, NZ + 4, forward_step, 0)
+        send_row(0)
+        weight_steps[3]()
+        attend(1, (0, 1))
+        lax.fori_loop(NZ + 4, NB, forward_step, 0)
+        weight_steps[4]()
+        weight_y2(0)
+        await_rows((2, 3))
+        attend(1, (2,), (2,))
+        finish(1)
+        attend(2, (1, 2, 3), (3,))
+        send_row(1)
+        finish(2)
+        weight_y2(1)
+        weight_y2(2)
+        attend(3, (2, 3))
+        send_row(2)
+        finish(3)
+        weight_y2(3)
+        send_row(3)
 
     def await_o(h, carry):
         await_copy(piece(attn, h), o_rcv.at[h])
@@ -334,16 +351,20 @@
         for n in range(4):
             await_copy(block(n, m, 1 - core), w5r.at[4 * m + n])
 
-    def drain_heads(i, carry):
-        h, to = head_of(i)
-
-        @pl.when(to != s)
-        def _():
-            for row, src, dst, rcv in streams:
-                remote(piece(src, h), dst.at[s], s_snd.at[row, h], rcv.at[s], (y, f, to)).wait_send()
-        return carry
-
-    lax.fori_loop(0, NH, drain_heads, 0)
+    def drain_heads(wave):
+        def step(i, carry):
+            h, to = head_of(wave, i)
+
+            @pl.when(to != s)
+            def _():
+                for row, src, dst, rcv in streams:
+                    remote(piece(src, h), dst.at[s], s_snd.at[row, h], rcv.at[s], (y, f, to)).wait_send()
+            return carry
+
+        lax.fori_loop(0, half, step, 0)
+
+    drain_heads(0)
+    drain_heads(1)
 
     def drain_w1(i, carry):
         w1(i).wait_send()
@@ -371,8 +392,8 @@
             return carry
 
         lax.fori_loop(0, NB, drain, 0)
-        for box in range(NB):
-            send_o(box, False)
+        for slot in range(NB):
+            send_o(slot, at_row(slot // GW) + slot % GW, False)
 
 
 def gather_and_attend(q, k, v, w):
@@ -382,7 +403,7 @@
         kernel,
         out_shape=(jax.ShapeDtypeStruct(q.shape, q.dtype),
                    jax.ShapeDtypeStruct((NF, NB) + w.shape, w.dtype)),
-        in_specs=[any_spec] * 4,
+        in_specs=[any_spec] * 3 + [pl.BlockSpec(memory_space=pltpu.VMEM)],
         out_specs=(any_spec, any_spec),
         scratch_shapes=[
             pltpu.VMEM((NB, ROWS, HD), jnp.bfloat16),

time: 89.8 us -> 95.8 us (1.067)
  the two profiles are of different devices: /device:TPU:3 before, /device:TPU:28 now
where the time goes in v4:
time: 95.8 us; the launch traced here: 95.7 us
  Pallas kernels  88.4 us (92%)
  matrix products  6.54 us (7%)
    pallas_call x1, Pallas kernels, gather_and_attend(): pl.pallas_call(kernel, out_shape=(jax.ShapeDtypeStruct(q.shape, q.dtype),...  88.4 us
    dot_general x1, matrix products, per_device(): jnp.dot(attention, weight.reshape(channels, width), preferred_element_typ...  6.54 us

profile of v4, /device:TPU:28, one launch (start us, length us, event | category | flops | bytes accessed | tf_op | source)
XLA Modules:
  0.0 95.7 jit_solution(12584021237721553246)
XLA Ops:
  0.0 0.0 copy-start
  0.0 0.8 convert_element_type.20
  0.8 88.4 %gather_and_attend.1 = (bf16[128,1536]{1,0:T(8,128)(2,1)}, bf16[4,16,24,3072]{3,2,1,0:T(8,128)(2,1)}) custom-call(bf16[128,1536]{1,0:T(8,128)(2,1)} %bitcast.16, bf16[128,1536]{1,0:T(8,128)(2,1)} %bitcast.17, bf16[128,1536]{1,0:T(8,128)(2,1)} %bitcast.18, bf16[24,3072]{1,0:T(8,128)(2,1)} %w_ref.1), custom_call_target="tpu_custom_call" | custom-call | tf_op jit(solution)/shard_map/gather_and_attend/pallas_call | solution.py:402
  89.2 0.0 copy-done
  89.2 6.5 %fusion.2 = bf16[128,3072]{1,0:T(8,128)(2,1)} fusion(bf16[128,1536]{1,0:T(8,128)(2,1)} %get-tuple-element.7, bf16[1536,3072]{1,0:T(8,128)(2,1)} %bitcast.13, bf16[128,3072]{1,0:T(8,128)(2,1)S(1)} %bitcast.14, bf16[128,3072]{1,0:T(8,128)(2,1)} %bitcast.15, f32[3072]{0:T(1024)S(1)} %convert_element_type.20), kind=kOutput, calls=%fused_computation.3 | convolution fusion | flops 1210318848 | bytes 12201984 | tf_op jit(solution)/shard_map/dot_general | solution.py:435
Async XLA Ops:
  0.0 89.2 %copy-start = (bf16[2,1,8,8,3072]{4,3,2,1,0:T(8,128)(2,1)S(1)}, bf16[2,1,8,8,3072]{4,3,2,1,0:T(8,128)(2,1)}, u32[]{:S(2)}) copy-start(bf16[2,1,8,8,3072]{4,3,2,1,0:T(8,128)(2,1)} %param.11) | copy-start | bytes 2359300

commit v5 on v3

--- a/solution.py
+++ b/solution.py
@@ -80,16 +80,18 @@
 
     first = jnp.minimum(my_head, NH - 1)
 
+    half = NH // 2
+
     def head_of(i):
-        h = (first + i) % NH
-        return h, (h // 3) * 4 + h % 3 + jnp.where((h >= NH // 2) & (h % 3 > 0), 1, 0)
+        h = ((lo + i // half) % 2) * half + (first + i) % half
+        return h, (h // 3) * 4 + h % 3 + jnp.where((h >= half) & (h % 3 > 0), 1, 0)
 
     def piece(ref, h):
         return ref.at[:, pl.ds(pl.multiple_of(h * HD, HD), HD)]
 
     streams = ((0, k_hbm, kbuf.at[0], k_rcv), (1, v_hbm, vbuf.at[0], v_rcv), (2, q_hbm, qbuf, q_rcv))
 
-    def send_heads(which):
+    def send_heads(which, i0=0, i1=NH):
         def step(i, carry):
             h, to = head_of(i)
             for n in which:
@@ -104,10 +106,8 @@
                     remote(piece(src, h), dst.at[s], s_snd.at[row, h], rcv.at[s], (y, f, to)).start()
             return carry
 
-        lax.fori_loop(0, NH, step, 0)
-
-    send_heads((0, 1))
-    send_heads((2,))
+        lax.fori_loop(i0, i1, step, 0)
+
 
     places = (x, xl, xr, (x + 2) % 4)
     layers = (y, yl, yr, (y + 2) % NY)
@@ -177,7 +177,7 @@
         return carry
 
     def forward(i):
-        box = (s + NB - i) % NB
+        box = ((lo + i // NZ) % 2) * NZ + (z + NB - i) % NZ
         out = []
         for n, (buf, rcv) in enumerate(((kbuf, k_rcv), (vbuf, v_rcv))):
             out.append((buf, rcv, box,
@@ -198,14 +198,17 @@
             near.start()
         return carry
 
-    weight_steps = (weight_z, weight_x, weight_x2) + tuple(functools.partial(weight_y, n) for n in range(4))
+    weight_z()
+    send_heads((0, 1))
+    send_heads((2,))
+    weight_steps = (weight_x, weight_x2) + tuple(functools.partial(weight_y, n) for n in range(4))
 
     @pl.when(owner)
     def _():
         mbuf[...] = jnp.full_like(mbuf, -1e30)
         lbuf[...] = jnp.zeros_like(lbuf)
         acc[...] = jnp.zeros_like(acc)
-        marks = (0, 2, 4, 6, 8, 11, 14, NB)
+        marks = (0, 0, 4, 8, 12, 14, NB)
         for step, i0, i1 in zip(weight_steps, marks, marks[1:]):
             step()
             lax.fori_loop(i0, i1, forward_step, 0)

time: 89.8 us -> 83.6 us (0.931)
  Pallas kernels: 82.4 us -> 76.1 us
    pallas_call x1, Pallas kernels: 82.4 us -> 76.1 us  [gather_and_attend(): pl.pallas_call(kernel, out_shape=(jax.ShapeDtypeStruct(q.shape, q.dtype),...]
where the time goes in v5:
time: 83.6 us; the launch traced here: 83.4 us
  Pallas kernels  76.1 us (91%)
  matrix products  6.54 us (8%)
    pallas_call x1, Pallas kernels, gather_and_attend(): pl.pallas_call(kernel, out_shape=(jax.ShapeDtypeStruct(q.shape, q.dtype),...  76.1 us
    dot_general x1, matrix products, per_device(): jnp.dot(attention, weight.reshape(channels, width), preferred_element_typ...  6.54 us

profile of v5, /device:TPU:3, one launch (start us, length us, event | category | flops | bytes accessed | tf_op | source)
XLA Modules:
  0.0 83.4 jit_solution(5074857778379600217)
XLA Ops:
  0.0 0.0 copy-start
  0.0 0.8 convert_element_type.20
  0.8 76.1 %gather_and_attend.1 = (bf16[128,1536]{1,0:T(8,128)(2,1)}, bf16[4,16,24,3072]{3,2,1,0:T(8,128)(2,1)}) custom-call(bf16[128,1536]{1,0:T(8,128)(2,1)} %bitcast.16, bf16[128,1536]{1,0:T(8,128)(2,1)} %bitcast.17, bf16[128,1536]{1,0:T(8,128)(2,1)} %bitcast.18, bf16[24,3072]{1,0:T(8,128)(2,1)} %w_hbm.1), custom_call_target="tpu_custom_call" | custom-call | tf_op jit(solution)/shard_map/gather_and_attend/pallas_call | solution.py:384
  76.9 0.0 copy-done
  76.9 6.5 %fusion.2 = bf16[128,3072]{1,0:T(8,128)(2,1)} fusion(bf16[128,1536]{1,0:T(8,128)(2,1)} %get-tuple-element.7, bf16[1536,3072]{1,0:T(8,128)(2,1)} %bitcast.13, bf16[128,3072]{1,0:T(8,128)(2,1)S(1)} %bitcast.14, bf16[128,3072]{1,0:T(8,128)(2,1)} %bitcast.15, f32[3072]{0:T(1024)S(1)} %convert_element_type.20), kind=kOutput, calls=%fused_computation.3 | convolution fusion | flops 1210318848 | bytes 12201984 | tf_op jit(solution)/shard_map/dot_general | solution.py:417
Async XLA Ops:
  0.0 76.9 %copy-start = (bf16[2,1,8,8,3072]{4,3,2,1,0:T(8,128)(2,1)S(1)}, bf16[2,1,8,8,3072]{4,3,2,1,0:T(8,128)(2,1)}, u32[]{:S(2)}) copy-start(bf16[2,1,8,8,3072]{4,3,2,1,0:T(8,128)(2,1)} %param.11) | copy-start | bytes 2359300
